TPU v7x, 512 devices: a whole 4x8x8 slice. The times are simulated.
512 devices in a mesh: row: 32 (over y_hi, z, core), col: 16 (over y_lo, x).
Axes of the slice: x: 4, y: 8 (y_hi: 2, y_lo: 4; y = y_hi * 4 + y_lo), z: 8, core: 2. Of those that a mesh axis runs over, the one named last changes fastest.
Arguments:
- stress: float32 [256, 16384], P('col', 'row'), may hold values from -2.5 to 2.5
- state: float32 [256, 8192], P('col', 'row'), may hold values from 0 to 1
- load_rate: int32 [256, 16384], P('col', 'row'), may hold values from 0 to 2047
- a_param: float32 [8192], P('row'), may hold values from 1 to 2
- b_param: float32 [8192], P('row'), may hold values from 0.25 to 1
- near_band: bfloat16 [16384, 768], P('row'), may hold values from -0.21875 to 0.21875
- u_far: bfloat16 [64, 64, 32, 256], P('row', 'col'), may hold values from -0.1875 to 0.1875
- v_far: bfloat16 [64, 64, 32, 256], P('row', 'col'), may hold values from -0.375 to 0.375
- ranks: int32 [64, 64], P('row', 'col'), may hold values from 1 to 32, as said below
Outputs:
- new_stress: float32 [256, 16384], P('col', 'row')
- new_state: float32 [256, 8192], P('col', 'row')
Inputs may be any that keep to these rules, and one draw needn't show every extreme that they name: ranks of blocks with |I - J| <= 1 are not used; blocks with |I - J| = 2 have rank 32.
All inputs are finite; a program needn't handle non-finite values.
Results may differ from a plain program's by a relative error of at most 0.0021.
Values may be sent and summed in bfloat16 or wider, within the bound.
No kernel may reach another device: no remote copies, remote signals or barrier semaphores. Data moves between devices by JAX's collectives and lax.ppermute only.
A program may use at most 64 MiB of HBM per device.

v0:
```python
import jax
import jax.numpy as jnp
from jax import lax
from jax.sharding import PartitionSpec as P

B = 128
HSTEP = 0.2
RATE_UNIT = 1.0 / 1024.0


def broadcast(value, axis, source):
    kept = jnp.where(lax.axis_index(axis) == source, value, 0).astype(value.dtype)
    return lax.psum(kept, axis)


def extended(cells, sides, width):
    for axis, dim in sides:
        count = lax.axis_size(axis)
        ends = count - 1
        head = lax.slice_in_dim(cells, 0, width, axis=dim)
        tail = lax.slice_in_dim(cells, cells.shape[dim] - width, cells.shape[dim], axis=dim)
        cells = jnp.concatenate(
            [
                lax.ppermute(tail, axis, [(i, (i + 1) % count) for i in range(ends)]),
                cells,
                lax.ppermute(head, axis, [((i + 1) % count, i) for i in range(ends)]),
            ],
            axis=dim,
        )
    return cells


def rates_and_drift(stress_now, state_now, plate_rate, a_param, b_param):
    members = stress_now.shape[0]
    block_count = a_param.shape[0] // B
    stress_view = stress_now.reshape(members, block_count, 2, B)
    state_view = state_now.reshape(members, block_count, 1, B)
    direct_view = a_param.reshape(1, block_count, 1, B)
    evolve_view = b_param.reshape(1, block_count, B)
    slip_rate = 2.0 * jnp.exp(-state_view) * jnp.sinh(stress_view / direct_view)
    slip_speed = jnp.sqrt(jnp.sum(slip_rate * slip_rate, axis=2))
    drift = evolve_view * (jnp.exp(-state_view[:, :, 0]) - slip_speed)
    excess = (slip_rate - plate_rate.reshape(members, block_count, 2, B)).astype(jnp.bfloat16)
    return (excess.reshape(members, -1), drift.reshape(members, -1))


def far_terms(columns, u_far, v_far, ranks, row_index, col_index):
    block_rows, block_cols, rank_slots, block_dofs = u_far.shape
    members = columns.shape[0]
    grid = columns.reshape(members, block_cols, block_dofs)
    weights = jnp.einsum("mjd,ijrd->ijmr", grid, v_far, preferred_element_type=jnp.float32)
    global_rows = row_index * block_rows + jnp.arange(block_rows, dtype=jnp.int32)
    global_cols = col_index * block_cols + jnp.arange(block_cols, dtype=jnp.int32)
    distant = jnp.abs(global_rows[:, None] - global_cols[None, :]) >= 2
    active = (jnp.arange(rank_slots, dtype=jnp.int32)[None, None, :] < ranks[:, :, None]) & distant[
        :, :, None
    ]
    weights = jnp.where(active[:, :, None, :], weights, 0.0).astype(jnp.bfloat16)
    partial_value = jnp.einsum("ijmr,ijrd->mid", weights, u_far, preferred_element_type=jnp.float32)
    return partial_value.reshape(members, -1)


def near_terms(padded, first_block, near_band):
    block_dofs = near_band.shape[1] // 3
    block_rows = near_band.shape[0] // block_dofs
    members = padded.shape[0]
    segment = lax.dynamic_slice_in_dim(
        padded, first_block * block_dofs, (block_rows + 2) * block_dofs, 1
    )
    segment = segment.reshape(members, block_rows + 2, block_dofs)
    windows = jnp.concatenate(
        [segment[:, 0:block_rows], segment[:, 1 : block_rows + 1], segment[:, 2 : block_rows + 2]],
        axis=2,
    )
    band_view = near_band.reshape(block_rows, block_dofs, 3 * block_dofs)
    nearby = jnp.einsum("mik,idk->mid", windows, band_view, preferred_element_type=jnp.float32)
    return nearby.reshape(members, -1)


def local(stress, state, load_rate, a_param, b_param, near_band, u_far, v_far, ranks):
    row_index = lax.axis_index("row")
    col_index = lax.axis_index("col")
    row_ratio = lax.axis_size("row") // lax.axis_size("col")
    block_rows = u_far.shape[0]
    block_dofs = near_band.shape[1] // 3
    plate_rate = load_rate.astype(jnp.float32) * RATE_UNIT
    stress_start, state_start = (stress, state)

    def tendency(stress_now, state_now):
        excess, drift = rates_and_drift(stress_now, state_now, plate_rate, a_param, b_param)
        all_members = lax.all_gather(excess, "col", axis=0, tiled=True)
        owners = []
        for offset in range(row_ratio):
            owners.append(broadcast(all_members, "row", row_ratio * col_index + offset))
        columns = jnp.concatenate(owners, axis=1)
        partial_value = far_terms(columns, u_far, v_far, ranks, row_index, col_index)
        padded = extended(columns, (("col", 1),), block_dofs)
        on_band = col_index == row_index // row_ratio
        first_block = row_index % row_ratio * block_rows
        partial_value = partial_value + lax.cond(
            on_band,
            lambda: near_terms(padded, first_block, near_band),
            lambda: jnp.zeros_like(partial_value),
        )
        totals = lax.psum_scatter(partial_value, "col", scatter_dimension=0, tiled=True)
        return (-totals, drift)

    rate_one, drift_one = tendency(stress_start, state_start)
    stress_one = stress_start + HSTEP * rate_one
    state_one = state_start + HSTEP * drift_one
    rate_two, drift_two = tendency(stress_one, state_one)
    stress_two = 0.75 * stress_start + 0.25 * (stress_one + HSTEP * rate_two)
    state_two = 0.75 * state_start + 0.25 * (state_one + HSTEP * drift_two)
    rate_three, drift_three = tendency(stress_two, state_two)
    new_stress = stress_start / 3.0 + 2.0 / 3.0 * (stress_two + HSTEP * rate_three)
    new_state = state_start / 3.0 + 2.0 / 3.0 * (state_two + HSTEP * drift_three)
    return (new_stress, new_state)


def solution(mesh):
    return jax.shard_map(
        local,
        mesh=mesh,
        in_specs=(
            P("col", "row"),
            P("col", "row"),
            P("col", "row"),
            P("row"),
            P("row"),
            P("row", None),
            P("row", "col", None, None),
            P("row", "col", None, None),
            P("row", "col"),
        ),
        out_specs=(P("col", "row"), P("col", "row")),
        check_vma=False,
    )
```

profile of v0, /device:TPU:64, one launch (start us, length us, event | category | flops | bytes accessed | tf_op | source)
XLA Modules:
  0.0 1475.0 jit_solution(9471608002866167742)
XLA Ops:
  7.2 0.7 fusion.75
  8.0 0.7 div.62
  8.7 0.8 fusion.59
  9.6 43.9 %all_gather.9 = bf16[256,512]{1,0:T(8,128)(2,1)S(1)} all-gather(bf16[16,512]{1,0:T(8,128)(2,1)S(1)} %fusion.59), channel_id=1, replica_groups=mesh['row'=32,'col'=16] {'col'}, dimensions={0}, use_global_device_ids=true | all-gather | bytes 278528 | tf_op jit(solution)/shard_map/all_gather | solution.py:91
  53.4 0.9 broadcast_select_fusion.5
  54.6 336.6 %all-reduce.11.cloned.1.call-done = (bf16[256,512]{1,0:T(8,128)(2,1)}, bf16[256,512]{1,0:T(8,128)(2,1)}) async-done(((bf16[256,512]{1,0:T(8,128)(2,1)}, bf16[256,512]{1,0:T(8,128)(2,1)}), (bf16[256,512]{1,0:T(8,128)(2,1)}, bf16[256,512]{1,0:T(8,128)(2,1)})) %all-reduce.11.cloned.1.call-update) | async-done | bytes 524304 | tf_op jit(solution)/shard_map/psum | solution.py:13
  391.1 0.9 slice.60
  392.1 0.9 slice.61
  393.0 1.1 pad_maximum_fusion.3
  394.1 3.4 collective-permute-start
  397.5 1.3 collective-permute-start.1
  398.8 0.4 reshape.192
  399.2 0.5 fusion.29
  399.9 0.6 collective-permute-done
  400.5 4.1 collective-permute-done.1
  404.9 0.9 add.112
  406.2 92.3 %reduce-scatter.4.cloned.1.call-done = f32[16,512]{1,0:T(8,128)} async-done(((f32[256,512]{1,0:T(8,128)}), f32[16,512]{1,0:T(8,128)}) %reduce-scatter.4.cloned.1.call-update) | async-done | bytes 32784 | tf_op jit(solution)/shard_map/reduce_scatter | solution.py:105
  498.5 0.8 fusion.58
  499.4 38.8 %all_gather.10 = bf16[256,512]{1,0:T(8,128)(2,1)S(1)} all-gather(bf16[16,512]{1,0:T(8,128)(2,1)S(1)} %get-tuple-element.58), channel_id=1, replica_groups=mesh['row'=32,'col'=16] {'col'}, dimensions={0}, use_global_device_ids=true | all-gather | bytes 278528 | tf_op jit(solution)/shard_map/all_gather | solution.py:91
  538.2 0.9 broadcast_select_fusion.4
  539.1 336.2 %all-reduce.9.cloned.1.call-done = (bf16[256,512]{1,0:T(8,128)(2,1)}, bf16[256,512]{1,0:T(8,128)(2,1)}) async-done(((bf16[256,512]{1,0:T(8,128)(2,1)}, bf16[256,512]{1,0:T(8,128)(2,1)}), (bf16[256,512]{1,0:T(8,128)(2,1)}, bf16[256,512]{1,0:T(8,128)(2,1)})) %all-reduce.9.cloned.1.call-update) | async-done | bytes 524304 | tf_op jit(solution)/shard_map/psum | solution.py:13
  875.3 0.9 slice.62
  876.2 0.9 slice.63
  877.1 1.1 pad_maximum_fusion.4
  878.2 3.4 collective-permute-start.2
  881.6 1.3 collective-permute-start.3
  882.9 0.4 reshape.194
  883.3 0.5 fusion.28
  884.0 0.7 collective-permute-done.2
  884.7 4.1 collective-permute-done.3
  888.9 0.9 add.115
  890.2 92.4 %reduce-scatter.6.cloned.1.call-done = f32[16,512]{1,0:T(8,128)} async-done(((f32[256,512]{1,0:T(8,128)}), f32[16,512]{1,0:T(8,128)}) %reduce-scatter.6.cloned.1.call-update) | async-done | bytes 32784 | tf_op jit(solution)/shard_map/reduce_scatter | solution.py:105
  982.7 0.8 fusion.57
  983.5 38.8 %all_gather.11 = bf16[256,512]{1,0:T(8,128)(2,1)S(1)} all-gather(bf16[16,512]{1,0:T(8,128)(2,1)S(1)} %get-tuple-element.56), channel_id=1, replica_groups=mesh['row'=32,'col'=16] {'col'}, dimensions={0}, use_global_device_ids=true | all-gather | bytes 278528 | tf_op jit(solution)/shard_map/all_gather | solution.py:91
  1022.3 0.9 broadcast_select_fusion.3
  1023.2 336.3 %all-reduce.7.cloned.1.call-done = (bf16[256,512]{1,0:T(8,128)(2,1)}, bf16[256,512]{1,0:T(8,128)(2,1)}) async-done(((bf16[256,512]{1,0:T(8,128)(2,1)}, bf16[256,512]{1,0:T(8,128)(2,1)}), (bf16[256,512]{1,0:T(8,128)(2,1)}, bf16[256,512]{1,0:T(8,128)(2,1)})) %all-reduce.7.cloned.1.call-update) | async-done | bytes 524304 | tf_op jit(solution)/shard_map/psum | solution.py:13
  1359.5 0.9 slice.64
  1360.5 0.9 slice.65
  1361.4 1.1 pad_maximum_fusion.5
  1362.5 3.4 collective-permute-start.4
  1365.9 1.3 collective-permute-start.5
  1367.5 0.5 fusion.27
  1368.3 0.7 collective-permute-done.4
  1368.9 4.1 collective-permute-done.5
  1373.2 0.9 add.120
  1374.3 0.6 fusion.64
  1375.0 91.8 %reduce-scatter.8.cloned.1.call-done = f32[16,512]{1,0:T(8,128)} async-done(((f32[256,512]{1,0:T(8,128)}), f32[16,512]{1,0:T(8,128)}) %reduce-scatter.8.cloned.1.call-update) | async-done | bytes 32784 | tf_op jit(solution)/shard_map/reduce_scatter | solution.py:105
  1466.7 1.4 multiply_add_fusion
  (79 shorter events, 2.9 us)
Async XLA Ops:
  7.2 392.0 %copy-start = (bf16[2,4,32,256]{3,2,1,0:T(8,128)(2,1)S(1)}, bf16[2,4,32,256]{3,2,1,0:T(8,128)(2,1)}, u32[]{:S(2)}) copy-start(bf16[2,4,32,256]{3,2,1,0:T(8,128)(2,1)} %param.21) | copy-start | bytes 393220
  7.2 384.0 %all-reduce.11.cloned.1.call-start = ((), (), s32[]{:S(2)}) async-start(), calls=%async_computation.8 | async-start | bytes 1048576 | tf_op jit(solution)/shard_map/psum | solution.py:13
  9.5 44.9 %copy-start.13 = (s32[2,4]{1,0:T(2,128)S(1)}, s32[2,4]{1,0:T(2,128)}, u32[]{:S(2)}) copy-start(s32[2,4]{1,0:T(2,128)} %param.23) | copy-start | bytes 100
  54.3 444.2 %reduce-scatter.4.cloned.1.call-start = ((), (), s32[]{:S(2)}) async-start(), calls=%async_computation.3 | async-start | bytes 557056 | tf_op jit(solution)/shard_map/reduce_scatter | solution.py:105
  393.0 6.2 copy-start.7
  394.1 6.4 collective-permute-start
  397.5 7.2 collective-permute-start.1
  399.7 5.0 copy-start.1
  399.7 5.0 copy-start.2
  399.9 4.8 copy-start.14
  404.8 1.0 copy-start.8
  404.8 1.0 copy-start.11
  404.8 1.2 copy-start.10
  404.9 1.2 copy-start.12
  405.8 92.8 %copy-start.9 = (s32[16,512]{1,0:T(8,128)S(1)}, s32[16,512]{1,0:T(8,128)}, u32[]{:S(2)}) copy-start(s32[16,512]{1,0:T(8,128)} %param.17) | copy-start | bytes 98308
  405.8 469.5 %all-reduce.9.cloned.1.call-start = ((), (), s32[]{:S(2)}) async-start(), calls=%async_computation.7 | async-start | bytes 1048576 | tf_op jit(solution)/shard_map/psum | solution.py:13
  539.1 443.6 %reduce-scatter.6.cloned.1.call-start = ((), (), s32[]{:S(2)}) async-start(), calls=%async_computation.4 | async-start | bytes 557056 | tf_op jit(solution)/shard_map/reduce_scatter | solution.py:105
  878.2 6.4 collective-permute-start.2
  881.6 7.2 collective-permute-start.3
  883.8 5.0 copy-start.5
  883.8 5.0 copy-start.6
  889.8 469.7 %all-reduce.7.cloned.1.call-start = ((), (), s32[]{:S(2)}) async-start(), calls=%async_computation.6 | async-start | bytes 1048576 | tf_op jit(solution)/shard_map/psum | solution.py:13
  1023.2 443.6 %reduce-scatter.8.cloned.1.call-start = ((), (), s32[]{:S(2)}) async-start(), calls=%async_computation.5 | async-start | bytes 557056 | tf_op jit(solution)/shard_map/reduce_scatter | solution.py:105
  1362.5 6.4 collective-permute-start.4
  1365.9 7.2 collective-permute-start.5
  1368.0 5.0 copy-start.3
  1368.0 5.0 copy-start.4
Sparse Core Ops, SparseCore 0:
  54.4 336.6 all-reduce.10
  405.9 92.5 reduce-scatter.3
  539.2 336.0 all-reduce.8
  890.0 92.6 reduce-scatter.5
  1023.3 336.2 all-reduce.6
  1374.2 92.4 reduce-scatter.7
where the time goes:
time: 1480 us; the launch traced here: 1470 us
  waiting for transfers between devices  1300 us (88%)
  blocking collectives  122 us (8%)
    psum x3, waiting for transfers between devices, broadcast(): return lax.psum(kept, axis)  1010 us
    reduce_scatter x3, waiting for transfers between devices, tendency(): lax.psum_scatter(partial_value, 'col', scatter_dimension=0, tiled=True)  277 us
    all_gather x3, blocking collectives, tendency(): all_members = lax.all_gather(excess, 'col', axis=0, tiled=True)  122 us
  transfers between devices with their start and end apart: 12, of which 12 were waited for; matrix products, arithmetic and copies ran while one was open for 0% of the time, Pallas kernels for 0%

commit v1 on v0

--- a/solution.py
+++ b/solution.py
@@ -88,7 +88,9 @@
 
     def tendency(stress_now, state_now):
         excess, drift = rates_and_drift(stress_now, state_now, plate_rate, a_param, b_param)
-        all_members = lax.all_gather(excess, "col", axis=0, tiled=True)
+        all_members = jnp.concatenate(
+            lax.all_to_all(jnp.stack([excess] * lax.axis_size("col")), "col", 0, 0), axis=0
+        )
         owners = []
         for offset in range(row_ratio):
             owners.append(broadcast(all_members, "row", row_ratio * col_index + offset))

time: 1480 us -> 1400 us (0.946)
  blocking collectives: 122 us -> 25.7 us
    all_gather x3 -> x0, blocking collectives: 122 us -> none  [tendency(): all_members = lax.all_gather(excess, 'col', axis=0, tiled=True)]
    all_to_all x0 -> x2, blocking collectives: none -> 25.7 us  [tendency(): lax.all_to_all(jnp.stack([excess] * lax.axis_size('col')), 'col', 0, 0)]
  transfers between devices with their start and end apart: 12 -> 13, of which waited for: 12 -> 13; matrix products, arithmetic and copies ran while one was open for 0% -> 0% of each run, Pallas kernels for 0% -> 0%
where the time goes in v1:
time: 1400 us
  waiting for transfers between devices  1310 us (94%)
  blocking collectives  25.7 us (2%)
  starting transfers between devices  21.8 us (2%)
  between operations  14.7 us (1%)
  other arithmetic  14.5 us (1%)
    psum x3, waiting for transfers between devices, broadcast(): return lax.psum(kept, axis)  1010 us
    reduce_scatter x3, waiting for transfers between devices, tendency(): lax.psum_scatter(partial_value, 'col', scatter_dimension=0, tiled=True)  277 us
  transfers between devices with their start and end apart: 13, of which 13 were waited for; matrix products, arithmetic and copies ran while one was open for 0% of the time, Pallas kernels for 0%

profile of v1, /device:TPU:64, one launch (start us, length us, event | category | flops | bytes accessed | tf_op | source)
XLA Modules:
  0.0 1396.7 jit_solution(2423876554976787005)
XLA Ops:
  7.2 0.8 fusion.69
  8.0 0.7 div.65
  8.7 0.8 fusion.53
  9.5 0.7 stack.9
  10.2 7.4 all-to-all-start
  17.8 10.6 all-to-all-done
  28.4 0.8 broadcast_select_fusion.5
  29.5 337.2 %all-reduce.11.cloned.1.call-done = (bf16[256,512]{1,0:T(8,128)(2,1)}, bf16[256,512]{1,0:T(8,128)(2,1)}) async-done(((bf16[256,512]{1,0:T(8,128)(2,1)}, bf16[256,512]{1,0:T(8,128)(2,1)}), (bf16[256,512]{1,0:T(8,128)(2,1)}, bf16[256,512]{1,0:T(8,128)(2,1)})) %all-reduce.11.cloned.1.call-update) | async-done | bytes 524304 | tf_op jit(solution)/shard_map/psum | solution.py:13
  366.7 0.9 slice.60
  367.6 0.9 slice.61
  368.5 1.1 pad_maximum_fusion.3
  369.6 3.5 collective-permute-start
  373.1 1.3 collective-permute-start.1
  374.7 0.4 fusion.29
  375.3 0.9 collective-permute-done
  376.2 4.1 collective-permute-done.1
  380.5 0.9 add.112
  381.8 92.4 %reduce-scatter.4.cloned.1.call-done = f32[16,512]{1,0:T(8,128)} async-done(((f32[256,512]{1,0:T(8,128)}), f32[16,512]{1,0:T(8,128)}) %reduce-scatter.4.cloned.1.call-update) | async-done | bytes 32784 | tf_op jit(solution)/shard_map/reduce_scatter | solution.py:107
  474.2 0.8 fusion.52
  475.1 12.8 all_to_all.15
  487.9 0.8 broadcast_select_fusion.4
  488.8 335.3 %all-reduce.9.cloned.1.call-done = (bf16[256,512]{1,0:T(8,128)(2,1)}, bf16[256,512]{1,0:T(8,128)(2,1)}) async-done(((bf16[256,512]{1,0:T(8,128)(2,1)}, bf16[256,512]{1,0:T(8,128)(2,1)}), (bf16[256,512]{1,0:T(8,128)(2,1)}, bf16[256,512]{1,0:T(8,128)(2,1)})) %all-reduce.9.cloned.1.call-update) | async-done | bytes 524304 | tf_op jit(solution)/shard_map/psum | solution.py:13
  824.1 0.9 slice.62
  825.1 0.9 slice.63
  826.0 1.1 pad_maximum_fusion.4
  827.1 3.4 collective-permute-start.2
  830.5 1.3 collective-permute-start.3
  832.0 0.4 fusion.28
  832.6 0.9 collective-permute-done.2
  833.5 4.1 collective-permute-done.3
  837.8 0.9 add.115
  839.1 92.4 %reduce-scatter.6.cloned.1.call-done = f32[16,512]{1,0:T(8,128)} async-done(((f32[256,512]{1,0:T(8,128)}), f32[16,512]{1,0:T(8,128)}) %reduce-scatter.6.cloned.1.call-update) | async-done | bytes 32784 | tf_op jit(solution)/shard_map/reduce_scatter | solution.py:107
  931.5 0.8 fusion.51
  932.4 12.8 all_to_all.16
  945.2 0.8 broadcast_select_fusion.3
  946.1 335.1 %all-reduce.7.cloned.1.call-done = (bf16[256,512]{1,0:T(8,128)(2,1)}, bf16[256,512]{1,0:T(8,128)(2,1)}) async-done(((bf16[256,512]{1,0:T(8,128)(2,1)}, bf16[256,512]{1,0:T(8,128)(2,1)}), (bf16[256,512]{1,0:T(8,128)(2,1)}, bf16[256,512]{1,0:T(8,128)(2,1)})) %all-reduce.7.cloned.1.call-update) | async-done | bytes 524304 | tf_op jit(solution)/shard_map/psum | solution.py:13
  1281.2 0.9 slice.64
  1282.1 0.9 slice.65
  1283.0 1.1 pad_maximum_fusion.5
  1284.1 3.4 collective-permute-start.4
  1287.5 1.3 collective-permute-start.5
  1289.0 0.4 fusion.27
  1289.6 0.9 collective-permute-done.4
  1290.5 4.1 collective-permute-done.5
  1294.8 0.9 add.120
  1295.9 0.6 fusion.58
  1296.6 91.8 %reduce-scatter.8.cloned.1.call-done = f32[16,512]{1,0:T(8,128)} async-done(((f32[256,512]{1,0:T(8,128)}), f32[16,512]{1,0:T(8,128)}) %reduce-scatter.8.cloned.1.call-update) | async-done | bytes 32784 | tf_op jit(solution)/shard_map/reduce_scatter | solution.py:107
  1388.4 1.4 multiply_add_fusion
  (87 shorter events, 3.2 us)
Async XLA Ops:
  7.2 367.5 %copy-start = (bf16[2,4,32,256]{3,2,1,0:T(8,128)(2,1)S(1)}, bf16[2,4,32,256]{3,2,1,0:T(8,128)(2,1)}, u32[]{:S(2)}) copy-start(bf16[2,4,32,256]{3,2,1,0:T(8,128)(2,1)} %param.21) | copy-start | bytes 393220
  10.2 18.1 %all-to-all-start = ((bf16[16,16,512]{2,1,0:T(8,128)(2,1)}), bf16[16,16,512]{2,1,0:T(8,128)(2,1)S(1)}, u32[]{:S(2)}, u32[]{:S(2)}) async-start(bf16[16,16,512]{2,1,0:T(8,128)(2,1)} %stack.9), calls=%async_computation | async-start | bytes 524288 | tf_op jit(solution)/shard_map/all_to_all | solution.py:92
  17.7 11.7 copy-start.13
  17.7 349.0 %all-reduce.11.cloned.1.call-start = ((), (), s32[]{:S(2)}) async-start(), calls=%async_computation.11 | async-start | bytes 1048576 | tf_op jit(solution)/shard_map/psum | solution.py:13
  29.2 445.0 %reduce-scatter.4.cloned.1.call-start = ((), (), s32[]{:S(2)}) async-start(), calls=%async_computation.6 | async-start | bytes 557056 | tf_op jit(solution)/shard_map/reduce_scatter | solution.py:107
  369.6 5.1 copy-start.7
  369.6 6.6 collective-permute-start
  373.1 7.2 collective-permute-start.1
  375.1 5.2 copy-start.1
  375.1 5.2 copy-start.2
  375.3 5.1 copy-start.14
  380.4 1.0 copy-start.8
  380.5 1.0 copy-start.11
  380.5 1.2 copy-start.10
  380.5 1.2 copy-start.12
  381.4 92.9 %copy-start.9 = (s32[16,512]{1,0:T(8,128)S(1)}, s32[16,512]{1,0:T(8,128)}, u32[]{:S(2)}) copy-start(s32[16,512]{1,0:T(8,128)} %param.17) | copy-start | bytes 98308
  381.4 442.7 %all-reduce.9.cloned.1.call-start = ((), (), s32[]{:S(2)}) async-start(), calls=%async_computation.10 | async-start | bytes 1048576 | tf_op jit(solution)/shard_map/psum | solution.py:13
  488.8 442.7 %reduce-scatter.6.cloned.1.call-start = ((), (), s32[]{:S(2)}) async-start(), calls=%async_computation.7 | async-start | bytes 557056 | tf_op jit(solution)/shard_map/reduce_scatter | solution.py:107
  827.1 6.4 collective-permute-start.2
  830.5 7.2 collective-permute-start.3
  832.4 5.3 copy-start.5
  832.4 5.2 copy-start.6
  832.6 5.1 copy-start.15
  838.7 442.5 %all-reduce.7.cloned.1.call-start = ((), (), s32[]{:S(2)}) async-start(), calls=%async_computation.9 | async-start | bytes 1048576 | tf_op jit(solution)/shard_map/psum | solution.py:13
  946.1 442.4 %reduce-scatter.8.cloned.1.call-start = ((), (), s32[]{:S(2)}) async-start(), calls=%async_computation.8 | async-start | bytes 557056 | tf_op jit(solution)/shard_map/reduce_scatter | solution.py:107
  1284.1 6.4 collective-permute-start.4
  1287.5 7.2 collective-permute-start.5
  1289.4 5.3 copy-start.3
  1289.4 5.2 copy-start.4
  1289.6 5.1 copy-start.16
Sparse Core Ops, SparseCore 0:
  29.4 337.2 all-reduce.10
  381.5 92.6 reduce-scatter.3
  488.9 335.1 all-reduce.8
  838.8 92.6 reduce-scatter.5
  946.2 334.9 all-reduce.6
  1295.8 92.5 reduce-scatter.7
